TPU v7x, 32 devices: a whole 2x2x4 slice. The times are simulated.
32 devices in a mesh: seg: 4 (over x, core), space: 8 (over z, y).
Axes of the slice: x: 2, y: 2, z: 4, core: 2. Of those that a mesh axis runs over, the one named last changes fastest.
Arguments:
- directions: float32 [4, 16, 32, 64, 128], P('seg', None, 'space'), may hold values from -100 to 100
- adjoint: float32 [4, 32, 64, 128], P('seg', 'space'), may hold values from -1000 to 1000
- velocity: float32 [4, 3, 32, 64, 128], P('seg', None, 'space'), may hold values from -1 to 1
- diffusivity: float32 [4, 32, 64, 128], P('seg', 'space'), may hold values from 0.05 to 0.15
- objective_source: float32 [4, 32, 64, 128], P('seg', 'space'), may hold values from -6 to 6
- segment_start: int32 [4], P('seg'), may hold values from 0 to 999
Outputs:
- basis_rows: float32 [4, 16, 32, 64, 128], P('seg', None, 'space')
- factor_upper: float32 [4, 16, 16], P('seg')
- coefficients: float32 [4, 16], P('seg')
- shadow: float32 [4, 32, 64, 128], P('seg', 'space')
- gradient: float32 [32, 64, 128], P('space', 'seg')
All inputs are finite; a program needn't handle non-finite values.
Results may differ from a plain program's by a relative error of at most 0.0003.
Values sent between devices are 32-bit elements; how exact they have to be, the bound alone decides.
No kernel may reach another device: no remote copies, remote signals or barrier semaphores. Data moves between devices by JAX's collectives and lax.ppermute only.
A program may use at most 64 MiB of HBM per device.

v0:
```python
import math
import jax
import jax.numpy as jnp
from jax import lax
from jax.sharding import PartitionSpec as P


def with_halo(array, sides, width):
    for axis, dim in sides:
        size, length = (lax.axis_size(axis), array.shape[dim])
        up = [(i, (i + 1) % size) for i in range(size)]
        down = [(j, i) for i, j in up]
        last = lax.slice_in_dim(array, length - width, length, axis=dim)
        first = lax.slice_in_dim(array, 0, width, axis=dim)
        before = lax.ppermute(last, axis, up)
        after = lax.ppermute(first, axis, down)
        array = jnp.concatenate([before, array, after], axis=dim)
    return array


def modulation(window_start, section):
    phase_step = (window_start + 2 - section) % 64
    return 1.0 + 0.5 * jnp.sin(2.0 * math.pi * phase_step.astype(jnp.float32) / 64.0)


def advance(extended, diffusivity, velocity, strength):
    middle = extended[:, 1:-1]
    forward_x = extended[:, 2:]
    behind_x = extended[:, :-2]
    wall_zero = jnp.zeros_like(middle[:, :, :1])
    forward_y = jnp.concatenate([middle[:, :, 1:], wall_zero], axis=2)
    behind_y = jnp.concatenate([wall_zero, middle[:, :, :-1]], axis=2)
    forward_z = jnp.roll(middle, -1, axis=3)
    behind_z = jnp.roll(middle, 1, axis=3)
    laplace = forward_x + behind_x + forward_y + behind_y + forward_z + behind_z - 6.0 * middle
    transport = (
        velocity[0] * (forward_x - behind_x)
        + velocity[1] * (forward_y - behind_y)
        + velocity[2] * (forward_z - behind_z)
    )
    return middle + diffusivity * laplace + 0.5 * strength * transport


def body(directions, adjoint, velocity, diffusivity, objective_source, segment_start):
    count_dirs = directions.shape[1]
    stacked = jnp.concatenate([directions[0], adjoint[0][None]], axis=0)
    flow = velocity[0]
    spread = diffusivity[0]
    source = objective_source[0]
    window_start = segment_start[0]
    first_adjoint = source
    for section in (1, 2):
        extended = with_halo(stacked, (("space", 1),), 1)
        stacked = advance(extended, spread, flow, modulation(window_start, section))
        stacked = stacked.at[-1].add(source)
        if section == 1:
            first_adjoint = stacked[-1]
    flattened = stacked.reshape(count_dirs + 1, -1)
    cell_count = flattened.shape[1] * lax.axis_size("space")
    partial_sums = jnp.dot(
        flattened[:count_dirs], flattened[:count_dirs].T, precision=lax.Precision.HIGHEST
    )
    summed = lax.psum(partial_sums, "space") / cell_count
    triangle = jnp.linalg.cholesky(summed)
    inverse = jax.scipy.linalg.solve_triangular(
        triangle, jnp.eye(count_dirs, dtype=triangle.dtype), lower=True
    )
    basis_rows = jnp.dot(inverse, flattened[:count_dirs], precision=lax.Precision.HIGHEST)
    local_along = jnp.dot(basis_rows, flattened[count_dirs], precision=lax.Precision.HIGHEST)
    coefficients = lax.psum(local_along, "space") / cell_count
    shadow = flattened[count_dirs] - jnp.dot(
        coefficients, basis_rows, precision=lax.Precision.HIGHEST
    )
    shadow = shadow.reshape(source.shape)
    gradient = lax.psum_scatter(first_adjoint + shadow, "seg", scatter_dimension=1, tiled=True)
    basis_out = basis_rows.reshape((1,) + directions.shape[1:])
    return (basis_out, triangle.T[None], coefficients[None], shadow[None], gradient)


def solution(mesh):
    return jax.shard_map(
        body,
        mesh=mesh,
        in_specs=(
            P("seg", None, "space", None, None),
            P("seg", "space", None, None),
            P("seg", None, "space", None, None),
            P("seg", "space", None, None),
            P("seg", "space", None, None),
            P("seg"),
        ),
        out_specs=(
            P("seg", None, "space", None, None),
            P("seg", None, None),
            P("seg", None),
            P("seg", "space", None, None),
            P("space", "seg", None),
        ),
        check_vma=False,
    )
```

profile of v0, /device:TPU:0, one launch (start us, length us, event | category | flops | bytes accessed | tf_op | source)
XLA Modules:
  0.0 164.7 jit_solution(1982176983148332593)
XLA Ops:
  7.2 0.0 copy-start.3
  7.2 0.0 reduce-scatter.2.cloned.1.call-start
  7.2 2.8 %copy.51 = f32[1,16,4,64,128]{4,1,3,2,0:T(8,128)S(1)} copy(f32[1,16,4,64,128]{4,3,2,1,0:T(8,128)} %param.10) | data formatting | bytes 4194304 | tf_op args[0]
  10.1 0.0 copy-start
  10.1 0.0 copy-done.3
  10.1 0.1 fusion.10
  10.2 0.1 copy.28
  10.3 6.1 %collective-permute-start = (f32[17,1,64,128]{3,2,1,0:T(8,128)S(1)}, f32[17,1,64,128]{3,2,1,0:T(8,128)}, u32[]{:S(2)}, u32[]{:S(2)}) collective-permute-start(f32[17,1,64,128]{3,2,1,0:T(8,128)S(1)} %copy.28), channel_id=1, source_target_pairs={{1,0},{2,1},{3,2},{4,3},{5,4},{6,5},{7,6},{0,7},{9,8},{10,9},{11,1... | collective-permute-start | bytes 1671176 | tf_op jit(solution)/shard_map/ppermute | solution.py:16
  16.4 0.9 copy.30
  17.3 0.0 collective-permute-start.1
  17.3 3.0 %fusion.4 = (f32[17,4,63,128]{3,0,2,1:T(8,128)}, f32[17,4,63,128]{3,0,2,1:T(8,128)}) fusion(f32[16,4,64,128]{3,0,2,1:T(8,128)S(1)} %bitcast.60, f32[1,4,64,128]{3,0,2,1:T(1,128)S(1)} %bitcast.67), kind=kLoop, calls=%fused_computation.33 | loop fusion | flops 1096704 | bytes 6615040 | tf_op jit(solution)/shard_map/concatenate | solution.py:46
  20.3 0.0 copy-done.12
  20.3 0.7 slice_bitcast_fusion.2
  21.8 1.0 fusion.1
  22.8 0.0 copy-done
  22.8 0.0 copy-start.2
  22.8 0.0 copy-start.4
  22.8 0.0 copy-start.8
  22.9 1.0 fusion
  23.9 0.0 copy-start.1
  23.9 14.1 %collective-permute-done = f32[17,1,64,128]{3,2,1,0:T(8,128)} collective-permute-done((f32[17,1,64,128]{3,2,1,0:T(8,128)S(1)}, f32[17,1,64,128]{3,2,1,0:T(8,128)}, u32[]{:S(2)}, u32[]{:S(2)}) %collective-permute-start) | collective-permute-done | bytes 557088 | tf_op jit(solution)/shard_map/ppermute | solution.py:16
  38.0 1.4 copy.29
  39.4 0.0 collective-permute-done.1
  39.4 1.4 copy.31
  40.9 0.0 copy-start.10
  40.9 5.5 %multiply_add_fusion.1 = f32[17,4,64,128]{3,0,2,1:T(8,128)S(1)} fusion(f32[1,4,64,128]{3,0,2,1:T(1,128)S(1)} %bitcast.70, f32[16,4,64,128]{3,0,2,1:T(8,128)S(1)} %bitcast.63, f32[17,4,64,127]{3,0,2,1:T(8,128)S(1)} %get-tuple-element.57, f32[17,4,64,1]{3,0,2,1:T(8,128)S(1)} %get-tuple-element.59, f32[17,4,64,1]{3,0,2,1:T(8,128)S(1)} %get-tuple-element.58, ...), kind=kLoop, calls=%fused_computation.32 | loop fusion | flops 14483456 | bytes 14938116 | tf_op jit(solution)/shard_map/add | solution.py:41
  46.4 0.0 copy-done.10
  46.4 0.1 slice_add_fusion.1
  46.6 2.6 %scatter-add.4 = f32[17,4,64,128]{3,0,2,1:T(8,128)S(1)} dynamic-update-slice(f32[17,4,64,128]{3,0,2,1:T(8,128)S(1)} %multiply_add_fusion.1, f32[1,4,64,128]{3,0,2,1:T(1,128)S(1)} %slice_add_fusion.1, s32[]{:T(128)} %constant.129.clone.1, s32[]{:T(128)} %constant.123.clone.1, s32[]{:T(128)} %constant.123.clone.1, s32[]{:T(128)} %constant.123.clone.1) | dynamic-update-slice | bytes 262148 | tf_op jit(solution)/shard_map/scatter-add | solution.py:55
  49.2 0.1 fusion.21
  49.3 1.0 fusion.24
  50.3 0.1 copy.35
  50.4 0.1 copy.33
  50.5 4.8 %collective-permute-start.2 = (f32[17,1,64,128]{3,2,1,0:T(8,128)S(1)}, f32[17,1,64,128]{3,2,1,0:T(8,128)S(1)}, u32[]{:S(2)}, u32[]{:S(2)}) collective-permute-start(f32[17,1,64,128]{3,2,1,0:T(8,128)S(1)} %copy.33), channel_id=1, source_target_pairs={{1,0},{2,1},{3,2},{4,3},{5,4},{6,5},{7,6},{0,7},{9,8},{10,9},{11,1... | collective-permute-start | bytes 1671176 | tf_op jit(solution)/shard_map/ppermute | solution.py:16
  55.4 0.0 collective-permute-start.3
  55.4 2.0 %fusion.22 = (f32[17,4,63,128]{3,0,2,1:T(8,128)S(1)}, f32[17,4,63,128]{3,0,2,1:T(8,128)}) fusion(f32[17,4,64,128]{3,0,2,1:T(8,128)S(1)} %scatter-add.4), kind=kLoop, calls=%fused_computation.68 | loop fusion | bytes 8773632 | tf_op jit(solution)/shard_map/slice | solution.py:31
  57.4 1.0 fusion.23
  58.4 18.2 %collective-permute-done.2 = f32[17,1,64,128]{3,2,1,0:T(8,128)S(1)} collective-permute-done((f32[17,1,64,128]{3,2,1,0:T(8,128)S(1)}, f32[17,1,64,128]{3,2,1,0:T(8,128)S(1)}, u32[]{:S(2)}, u32[]{:S(2)}) %collective-permute-start.2) | collective-permute-done | bytes 557088 | tf_op jit(solution)/shard_map/ppermute | solution.py:16
  76.6 1.2 copy.34
  77.8 0.0 collective-permute-done.3
  77.8 1.2 copy.36
  79.0 5.9 %multiply_add_fusion = f32[17,4,64,128]{3,0,2,1:T(8,128)S(1)} fusion(f32[17,4,64,128]{3,0,2,1:T(8,128)S(1)} %scatter-add.4, f32[17,4,64,127]{3,0,2,1:T(8,128)S(1)} %get-tuple-element.49, f32[17,4,64,1]{3,0,2,1:T(8,128)S(1)} %get-tuple-element.51, f32[17,4,64,1]{3,0,2,1:T(8,128)S(1)} %get-tuple-element.50, f32[17,4,64,127]{3,0,2,1:T(8,128)S(1)} %get-tuple-element.48, ...), kind=kLoop, calls=%fused_computation.31 | loop fusion | flops 12812288 | bytes 14938116 | tf_op jit(solution)/shard_map/add | solution.py:41
  84.9 2.9 %convolution_bitcast_fusion = f32[16,16]{0,1:T(8,128)S(1)} fusion(f32[17,4,64,128]{3,0,2,1:T(8,128)S(1)} %multiply_add_fusion), kind=kOutput, calls=%fused_computation.39 | convolution fusion | flops 100663296 | bytes 2098176 | tf_op jit(solution)/shard_map/dot_general | solution.py:60
  87.8 1.1 slice_add_fusion
  88.8 0.2 slice.213
  89.0 20.7 %psum.14 = f32[16,16]{0,1:T(8,128)S(1)} all-reduce(f32[16,16]{0,1:T(8,128)S(1)} %convolution_bitcast_fusion), channel_id=1, replica_groups=mesh['seg'=4,'space'=8] {'space'}, use_global_device_ids=true, to_apply=%region_0.1 | all-reduce | flops 256 | bytes 2048 | tf_op jit(solution)/shard_map/psum | solution.py:63
  109.7 0.1 copy.38
  109.8 1.5 cholesky.17
  111.3 0.6 compare_reduce_fusion
  111.9 0.6 fusion.14
  112.6 1.2 custom-call.7
  113.8 0.2 fusion.11
  114.0 0.7 copy.39
  114.7 2.8 %fusion.6 = f32[16,32768]{1,0:T(8,128)S(1)} fusion(f32[16,16]{1,0:T(8,128)S(1)} %fusion.11, f32[2,8,256,128]{3,2,1,0:T(8,128)S(1)} %bitcast.65), kind=kOutput, calls=%fused_computation.35 | convolution fusion | flops 100663296 | bytes 4195328 | tf_op jit(solution)/shard_map/dot_general | solution.py:68
  117.6 2.6 %convolution_bitcast_fusion.1 = f32[16]{0:T(128)S(1)} fusion(f32[16,32768]{1,0:T(8,128)S(1)} %fusion.6, f32[32768,1]{0,1:T(1,128)S(1)} %bitcast.72), kind=kOutput, calls=%fused_computation.40 | convolution fusion | flops 6291456 | bytes 2228288 | tf_op jit(solution)/shard_map/dot_general | solution.py:69
  120.1 17.1 %psum.15 = f32[16]{0:T(128)S(1)} all-reduce(f32[16]{0:T(128)S(1)} %convolution_bitcast_fusion.1), channel_id=1, replica_groups=mesh['seg'=4,'space'=8] {'space'}, use_global_device_ids=true, to_apply=%region_3.4 | all-reduce | flops 16 | bytes 128 | tf_op jit(solution)/shard_map/psum | solution.py:70
  137.3 1.1 fusion.15
  138.4 0.0 copy-start.11
  138.4 0.7 add.143
  139.1 0.0 reduce-scatter.2.cloned.1.call-update
  139.1 0.7 copy.41
  139.8 1.7 %copy.45 = f32[2,8,256,128]{3,2,1,0:T(8,128)} copy(f32[2,8,256,128]{3,1,2,0:T(8,128)S(1)} %bitcast.64) | data formatting | bytes 4194304
  141.5 0.5 multiply_bitcast_fusion
  142.0 15.8 %reduce-scatter.2.cloned.1.call-done = f32[4,16,128]{2,1,0:T(8,128)} async-done(((f32[4,64,128]{2,1,0:T(8,128)}), f32[4,16,128]{2,1,0:T(8,128)}) %reduce-scatter.2.cloned.1.call-update) | async-done | bytes 32784 | tf_op jit(solution)/shard_map/reduce_scatter | solution.py:75
  (18 shorter events, 0.1 us)
Async XLA Ops:
  7.2 2.9 %copy-start.3 = (f32[1,4,64,128]{3,2,1,0:T(8,128)S(1)}, f32[1,4,64,128]{3,2,1,0:T(8,128)}, u32[]{:S(2)}) copy-start(f32[1,4,64,128]{3,2,1,0:T(8,128)} %param.11) | copy-start | bytes 393220
  7.2 150.7 %reduce-scatter.2.cloned.1.call-start = ((), (), s32[]{:S(2)}) async-start(), calls=%async_computation.1 | async-start | bytes 163840 | tf_op jit(solution)/shard_map/reduce_scatter | solution.py:75
  10.1 12.7 %copy-start = (f32[1,16,4,64,128]{4,1,3,2,0:T(8,128)}, f32[1,16,4,64,128]{4,1,3,2,0:T(8,128)S(1)}, u32[]{:S(2)}) copy-start(f32[1,16,4,64,128]{4,1,3,2,0:T(8,128)S(1)} %copy.51) | copy-start | bytes 6291460
  10.3 27.7 %collective-permute-start = (f32[17,1,64,128]{3,2,1,0:T(8,128)S(1)}, f32[17,1,64,128]{3,2,1,0:T(8,128)}, u32[]{:S(2)}, u32[]{:S(2)}) collective-permute-start(f32[17,1,64,128]{3,2,1,0:T(8,128)S(1)} %copy.28), channel_id=1, source_target_pairs={{1,0},{2,1},{3,2},{4,3},{5,4},{6,5},{7,6},{0,7},{9,8},{10,9},{11,1... | collective-permute-start | bytes 1671176 | tf_op jit(solution)/shard_map/ppermute | solution.py:16
  17.3 3.0 %copy-start.12 = (f32[1,3,4,64,128]{4,3,2,1,0:T(8,128)S(1)}, f32[1,3,4,64,128]{4,3,2,1,0:T(8,128)}, u32[]{:S(2)}) copy-start(f32[1,3,4,64,128]{4,3,2,1,0:T(8,128)} %param.12) | copy-start | bytes 1179652
  17.3 22.1 %collective-permute-start.1 = (f32[17,1,64,128]{3,2,1,0:T(8,128)}, f32[17,1,64,128]{3,2,1,0:T(8,128)}, u32[]{:S(2)}, u32[]{:S(2)}) collective-permute-start(f32[17,1,64,128]{3,2,1,0:T(8,128)} %copy.30), channel_id=1, source_target_pairs={{0,1},{1,2},{2,3},{3,4},{4,5},{5,6},{6,7},{7,0},{8,9},{9,10},{10,1... | collective-permute-start | bytes 1671176 | tf_op jit(solution)/shard_map/ppermute | solution.py:15
  22.8 18.0 %copy-start.2 = (f32[17,4,63,128]{3,0,2,1:T(8,128)S(1)}, f32[17,4,63,128]{3,0,2,1:T(8,128)}, u32[]{:S(2)}) copy-start(f32[17,4,63,128]{3,0,2,1:T(8,128)} %get-tuple-element.54) | copy-start | bytes 6580228
  22.8 18.0 %copy-start.4 = (f32[4,64,128]{2,1,0:T(8,128)S(1)}, f32[4,64,128]{2,1,0:T(8,128)}, u32[]{:S(2)}) copy-start(f32[4,64,128]{2,1,0:T(8,128)} %get-tuple-element.62) | copy-start | bytes 393220
  22.8 18.0 %copy-start.8 = (f32[1,4,64,128]{3,2,1,0:T(8,128)S(1)}, f32[1,4,64,128]{3,2,1,0:T(8,128)}, u32[]{:S(2)}) copy-start(f32[1,4,64,128]{3,2,1,0:T(8,128)} %param.13) | copy-start | bytes 393220
  23.9 17.0 %copy-start.1 = (f32[1,16,4,64,128]{4,1,3,2,0:T(8,128)S(1)}, f32[1,16,4,64,128]{4,1,3,2,0:T(8,128)}, u32[]{:S(2)}) copy-start(f32[1,16,4,64,128]{4,1,3,2,0:T(8,128)} %copy-done) | copy-start | bytes 6291460
  40.9 5.6 %copy-start.10 = (f32[1,4,64,128]{3,2,1,0:T(8,128)S(1)}, f32[1,4,64,128]{3,2,1,0:T(8,128)}, u32[]{:S(2)}) copy-start(f32[1,4,64,128]{3,2,1,0:T(8,128)} %param.14) | copy-start | bytes 393220
  46.6 3.7 %copy-start.6 = (f32[1,4,64,128]{3,0,2,1:T(1,128)}, f32[1,4,64,128]{3,0,2,1:T(1,128)S(1)}, u32[]{:S(2)}) copy-start(f32[1,4,64,128]{3,0,2,1:T(1,128)S(1)} %slice_add_fusion.1) | copy-start | bytes 393220
  50.5 26.0 %collective-permute-start.2 = (f32[17,1,64,128]{3,2,1,0:T(8,128)S(1)}, f32[17,1,64,128]{3,2,1,0:T(8,128)S(1)}, u32[]{:S(2)}, u32[]{:S(2)}) collective-permute-start(f32[17,1,64,128]{3,2,1,0:T(8,128)S(1)} %copy.33), channel_id=1, source_target_pairs={{1,0},{2,1},{3,2},{4,3},{5,4},{6,5},{7,6},{0,7},{9,8},{10,9},{11,1... | collective-permute-start | bytes 1671176 | tf_op jit(solution)/shard_map/ppermute | solution.py:16
  55.4 22.4 %collective-permute-start.3 = (f32[17,1,64,128]{3,2,1,0:T(8,128)S(1)}, f32[17,1,64,128]{3,2,1,0:T(8,128)S(1)}, u32[]{:S(2)}, u32[]{:S(2)}) collective-permute-start(f32[17,1,64,128]{3,2,1,0:T(8,128)S(1)} %copy.35), channel_id=1, source_target_pairs={{0,1},{1,2},{2,3},{3,4},{4,5},{5,6},{6,7},{7,0},{8,9},{9,10},{10,1... | collective-permute-start | bytes 1671176 | tf_op jit(solution)/shard_map/ppermute | solution.py:15
  57.4 21.7 %copy-start.5 = (f32[4,64,128]{2,1,0:T(8,128)S(1)}, f32[4,64,128]{2,1,0:T(8,128)}, u32[]{:S(2)}) copy-start(f32[4,64,128]{2,1,0:T(8,128)} %get-tuple-element.62) | copy-start | bytes 393220
  57.4 21.7 %copy-start.9 = (f32[1,4,64,128]{3,2,1,0:T(8,128)S(1)}, f32[1,4,64,128]{3,2,1,0:T(8,128)}, u32[]{:S(2)}) copy-start(f32[1,4,64,128]{3,2,1,0:T(8,128)} %param.13) | copy-start | bytes 393220
  117.6 20.9 %copy-start.7 = (f32[1,4,64,128]{3,0,2,1:T(1,128)S(1)}, f32[1,4,64,128]{3,0,2,1:T(1,128)}, u32[]{:S(2)}) copy-start(f32[1,4,64,128]{3,0,2,1:T(1,128)} %copy-done.6) | copy-start | bytes 393220
  138.4 19.4 %copy-start.11 = (f32[32768]{0:T(1024)}, f32[32768]{0:T(1024)S(1)}, u32[]{:S(2)}) copy-start(f32[32768]{0:T(1024)S(1)} %sub.40) | copy-start | bytes 393220
Sparse Core Ops, SparseCore 0:
  139.3 18.5 reduce-scatter.1
where the time goes:
time: 165 us
  waiting for transfers between devices  48.1 us (29%)
  blocking collectives  37.8 us (23%)
  other arithmetic  22.9 us (14%)
  local copies, waits for them, and re-layouts  20.1 us (12%)
  between operations  15.2 us (9%)
  starting transfers between devices  11 us (7%)
  matrix products  9.58 us (6%)
    ppermute x2, waiting for transfers between devices, with_halo(): after = lax.ppermute(first, axis, down)  32.3 us
    psum x1, blocking collectives, body(): summed = lax.psum(partial_sums, 'space') / cell_count  20.7 us
    psum x1, blocking collectives, body(): coefficients = lax.psum(local_along, 'space') / cell_count  17.1 us
    reduce_scatter x1, waiting for transfers between devices, body(): lax.psum_scatter(first_adjoint + shadow, 'seg', scatter_dimension=1, tile...  15.8 us
    add x2, other arithmetic, advance(): return middle + diffusivity * laplace + 0.5 * strength * transport  11.4 us
    ppermute x2, starting transfers between devices, with_halo(): after = lax.ppermute(first, axis, down)  10.9 us
    unnamed x29, local copies, waits for them, and re-layouts  5.3 us
    concatenate x4, other arithmetic, body(): stacked = jnp.concatenate([directions[0], adjoint[0][None]], axis=0)  5.09 us
  transfers between devices with their start and end apart: 5, of which 3 were waited for; matrix products, arithmetic and copies ran while one was open for 9% of the time, Pallas kernels for 0%

commit v1 on v0

--- a/solution.py
+++ b/solution.py
@@ -60,7 +60,7 @@
     partial_sums = jnp.dot(
         flattened[:count_dirs], flattened[:count_dirs].T, precision=lax.Precision.HIGHEST
     )
-    summed = lax.psum(partial_sums, "space") / cell_count
+    summed = jnp.sum(lax.all_gather(partial_sums, "space"), axis=0) / cell_count
     triangle = jnp.linalg.cholesky(summed)
     inverse = jax.scipy.linalg.solve_triangular(
         triangle, jnp.eye(count_dirs, dtype=triangle.dtype), lower=True

time: 165 us -> 177 us (1.073)
  blocking collectives: 37.8 us -> 51.1 us
    all_gather x0 -> x1, blocking collectives: none -> 30.6 us  [body(): summed = jnp.sum(lax.all_gather(partial_sums, 'space'), axis=0) / cell_count]
    psum x1 -> x0, blocking collectives: 20.7 us -> none  [body(): summed = lax.psum(partial_sums, 'space') / cell_count]
    psum x1, blocking collectives: 17.1 us -> 20.6 us  [body(): coefficients = lax.psum(local_along, 'space') / cell_count]
where the time goes in v1:
time: 177 us; the launch traced here: 176 us
  blocking collectives  51.1 us (29%)
  waiting for transfers between devices  46.5 us (26%)
  other arithmetic  22.9 us (13%)
  local copies, waits for them, and re-layouts  20.1 us (11%)
  between operations  15.2 us (9%)
  starting transfers between devices  11 us (6%)
  matrix products  9.64 us (5%)
    ppermute x2, waiting for transfers between devices, with_halo(): after = lax.ppermute(first, axis, down)  32.3 us
    all_gather x1, blocking collectives, body(): summed = jnp.sum(lax.all_gather(partial_sums, 'space'), axis=0) / cell_count  30.6 us
    psum x1, blocking collectives, body(): coefficients = lax.psum(local_along, 'space') / cell_count  20.6 us
    reduce_scatter x1, waiting for transfers between devices, body(): lax.psum_scatter(first_adjoint + shadow, 'seg', scatter_dimension=1, tile...  14.1 us
    add x2, other arithmetic, advance(): return middle + diffusivity * laplace + 0.5 * strength * transport  11.4 us
    ppermute x2, starting transfers between devices, with_halo(): after = lax.ppermute(first, axis, down)  10.9 us
    unnamed x29, local copies, waits for them, and re-layouts  5.3 us
    concatenate x4, other arithmetic, body(): stacked = jnp.concatenate([directions[0], adjoint[0][None]], axis=0)  5.09 us
  transfers between devices with their start and end apart: 5, of which 3 were waited for; matrix products, arithmetic and copies ran while one was open for 9% of the time, Pallas kernels for 0%

profile of v1, /device:TPU:0, one launch (start us, length us, event | category | flops | bytes accessed | tf_op | source)
XLA Modules:
  0.0 176.4 jit_solution(8554309673470362384)
XLA Ops:
  7.2 0.0 copy-start.3
  7.2 0.0 reduce-scatter.2.cloned.1.call-start
  7.2 2.8 %copy.47 = f32[1,16,4,64,128]{4,1,3,2,0:T(8,128)S(1)} copy(f32[1,16,4,64,128]{4,3,2,1,0:T(8,128)} %param.10) | data formatting | bytes 4194304 | tf_op args[0]
  10.1 0.0 copy-start
  10.1 0.0 copy-done.3
  10.1 0.1 fusion.10
  10.2 0.1 copy.26
  10.3 6.1 %collective-permute-start = (f32[17,1,64,128]{3,2,1,0:T(8,128)S(1)}, f32[17,1,64,128]{3,2,1,0:T(8,128)}, u32[]{:S(2)}, u32[]{:S(2)}) collective-permute-start(f32[17,1,64,128]{3,2,1,0:T(8,128)S(1)} %copy.26), channel_id=1, source_target_pairs={{1,0},{2,1},{3,2},{4,3},{5,4},{6,5},{7,6},{0,7},{9,8},{10,9},{11,1... | collective-permute-start | bytes 1671176 | tf_op jit(solution)/shard_map/ppermute | solution.py:16
  16.4 0.9 copy.28
  17.3 0.0 collective-permute-start.1
  17.3 3.0 %fusion.4 = (f32[17,4,63,128]{3,0,2,1:T(8,128)}, f32[17,4,63,128]{3,0,2,1:T(8,128)}) fusion(f32[16,4,64,128]{3,0,2,1:T(8,128)S(1)} %bitcast.63, f32[1,4,64,128]{3,0,2,1:T(1,128)S(1)} %bitcast.70), kind=kLoop, calls=%fused_computation.33 | loop fusion | flops 1096704 | bytes 6615040 | tf_op jit(solution)/shard_map/concatenate | solution.py:46
  20.3 0.0 copy-done.12
  20.3 0.7 slice_bitcast_fusion.2
  21.8 1.0 fusion.1
  22.8 0.0 copy-done
  22.8 0.0 copy-start.2
  22.8 0.0 copy-start.4
  22.8 0.0 copy-start.8
  22.9 1.0 fusion
  23.9 0.0 copy-start.1
  23.9 14.1 %collective-permute-done = f32[17,1,64,128]{3,2,1,0:T(8,128)} collective-permute-done((f32[17,1,64,128]{3,2,1,0:T(8,128)S(1)}, f32[17,1,64,128]{3,2,1,0:T(8,128)}, u32[]{:S(2)}, u32[]{:S(2)}) %collective-permute-start) | collective-permute-done | bytes 557088 | tf_op jit(solution)/shard_map/ppermute | solution.py:16
  38.0 1.4 copy.27
  39.4 0.0 collective-permute-done.1
  39.4 1.4 copy.29
  40.9 0.0 copy-start.10
  40.9 5.5 %multiply_add_fusion.1 = f32[17,4,64,128]{3,0,2,1:T(8,128)S(1)} fusion(f32[1,4,64,128]{3,0,2,1:T(1,128)S(1)} %bitcast.73, f32[16,4,64,128]{3,0,2,1:T(8,128)S(1)} %bitcast.66, f32[17,4,64,127]{3,0,2,1:T(8,128)S(1)} %get-tuple-element.57, f32[17,4,64,1]{3,0,2,1:T(8,128)S(1)} %get-tuple-element.59, f32[17,4,64,1]{3,0,2,1:T(8,128)S(1)} %get-tuple-element.58, ...), kind=kLoop, calls=%fused_computation.32 | loop fusion | flops 14483456 | bytes 14938116 | tf_op jit(solution)/shard_map/add | solution.py:41
  46.4 0.0 copy-done.10
  46.4 0.1 slice_add_fusion.1
  46.6 2.6 %scatter-add.4 = f32[17,4,64,128]{3,0,2,1:T(8,128)S(1)} dynamic-update-slice(f32[17,4,64,128]{3,0,2,1:T(8,128)S(1)} %multiply_add_fusion.1, f32[1,4,64,128]{3,0,2,1:T(1,128)S(1)} %slice_add_fusion.1, s32[]{:T(128)} %constant.131.clone.1, s32[]{:T(128)} %constant.125.clone.1, s32[]{:T(128)} %constant.125.clone.1, s32[]{:T(128)} %constant.125.clone.1) | dynamic-update-slice | bytes 262148 | tf_op jit(solution)/shard_map/scatter-add | solution.py:55
  49.2 0.1 fusion.21
  49.3 1.0 fusion.24
  50.3 0.1 copy.33
  50.4 0.1 copy.31
  50.5 4.8 %collective-permute-start.2 = (f32[17,1,64,128]{3,2,1,0:T(8,128)S(1)}, f32[17,1,64,128]{3,2,1,0:T(8,128)S(1)}, u32[]{:S(2)}, u32[]{:S(2)}) collective-permute-start(f32[17,1,64,128]{3,2,1,0:T(8,128)S(1)} %copy.31), channel_id=1, source_target_pairs={{1,0},{2,1},{3,2},{4,3},{5,4},{6,5},{7,6},{0,7},{9,8},{10,9},{11,1... | collective-permute-start | bytes 1671176 | tf_op jit(solution)/shard_map/ppermute | solution.py:16
  55.4 0.0 collective-permute-start.3
  55.4 2.0 %fusion.22 = (f32[17,4,63,128]{3,0,2,1:T(8,128)S(1)}, f32[17,4,63,128]{3,0,2,1:T(8,128)}) fusion(f32[17,4,64,128]{3,0,2,1:T(8,128)S(1)} %scatter-add.4), kind=kLoop, calls=%fused_computation.67 | loop fusion | bytes 8773632 | tf_op jit(solution)/shard_map/slice | solution.py:31
  57.4 1.0 fusion.23
  58.4 18.2 %collective-permute-done.2 = f32[17,1,64,128]{3,2,1,0:T(8,128)S(1)} collective-permute-done((f32[17,1,64,128]{3,2,1,0:T(8,128)S(1)}, f32[17,1,64,128]{3,2,1,0:T(8,128)S(1)}, u32[]{:S(2)}, u32[]{:S(2)}) %collective-permute-start.2) | collective-permute-done | bytes 557088 | tf_op jit(solution)/shard_map/ppermute | solution.py:16
  76.6 1.2 copy.32
  77.8 0.0 collective-permute-done.3
  77.8 1.2 copy.34
  79.0 5.9 %multiply_add_fusion = f32[17,4,64,128]{3,0,2,1:T(8,128)S(1)} fusion(f32[17,4,64,128]{3,0,2,1:T(8,128)S(1)} %scatter-add.4, f32[17,4,64,127]{3,0,2,1:T(8,128)S(1)} %get-tuple-element.49, f32[17,4,64,1]{3,0,2,1:T(8,128)S(1)} %get-tuple-element.51, f32[17,4,64,1]{3,0,2,1:T(8,128)S(1)} %get-tuple-element.50, f32[17,4,64,127]{3,0,2,1:T(8,128)S(1)} %get-tuple-element.48, ...), kind=kLoop, calls=%fused_computation.31 | loop fusion | flops 12812288 | bytes 14938116 | tf_op jit(solution)/shard_map/add | solution.py:41
  84.9 2.9 %convolution_bitcast_fusion = f32[16,16]{1,0:T(8,128)S(1)} fusion(f32[17,4,64,128]{3,0,2,1:T(8,128)S(1)} %multiply_add_fusion), kind=kOutput, calls=%fused_computation.39 | convolution fusion | flops 100663296 | bytes 2098176 | tf_op jit(solution)/shard_map/dot_general | solution.py:60
  87.8 1.1 slice_add_fusion
  88.9 0.2 slice.213
  89.1 30.6 %all-gather = f32[128,16]{1,0:T(8,128)S(1)} all-gather(f32[16,16]{1,0:T(8,128)S(1)} %convolution_bitcast_fusion), channel_id=2, replica_groups=mesh['seg'=4,'space'=8] {'space'}, dimensions={0}, use_global_device_ids=true | all-gather | bytes 9216 | tf_op jit(solution)/shard_map/all_gather | solution.py:63
  119.7 0.1 copy.35
  119.7 1.5 cholesky.17
  121.2 0.6 compare_reduce_fusion
  121.9 0.6 fusion.14
  122.5 1.2 custom-call.7
  123.8 0.2 fusion.11
  124.0 0.7 copy.36
  124.7 2.8 %fusion.6 = f32[16,32768]{1,0:T(8,128)S(1)} fusion(f32[16,16]{1,0:T(8,128)S(1)} %fusion.11, f32[2,8,256,128]{3,2,1,0:T(8,128)S(1)} %bitcast.68), kind=kOutput, calls=%fused_computation.35 | convolution fusion | flops 100663296 | bytes 4195328 | tf_op jit(solution)/shard_map/dot_general | solution.py:68
  127.5 2.6 %convolution_bitcast_fusion.1 = f32[16]{0:T(128)S(1)} fusion(f32[16,32768]{1,0:T(8,128)S(1)} %fusion.6, f32[32768,1]{0,1:T(1,128)S(1)} %bitcast.75), kind=kOutput, calls=%fused_computation.40 | convolution fusion | flops 6291456 | bytes 2228288 | tf_op jit(solution)/shard_map/dot_general | solution.py:69
  130.1 20.6 %psum.7 = f32[16]{0:T(128)S(1)} all-reduce(f32[16]{0:T(128)S(1)} %convolution_bitcast_fusion.1), channel_id=1, replica_groups=mesh['seg'=4,'space'=8] {'space'}, use_global_device_ids=true, to_apply=%region_3.4 | all-reduce | flops 16 | bytes 128 | tf_op jit(solution)/shard_map/psum | solution.py:70
  150.6 1.1 fusion.15
  151.8 0.0 copy-start.11
  151.8 0.7 add.139
  152.5 0.0 reduce-scatter.2.cloned.1.call-update
  152.5 0.7 copy.38
  153.2 1.7 copy.41
  154.9 0.5 multiply_bitcast_fusion
  155.4 14.1 %reduce-scatter.2.cloned.1.call-done = f32[4,16,128]{2,1,0:T(8,128)} async-done(((f32[4,64,128]{2,1,0:T(8,128)}), f32[4,16,128]{2,1,0:T(8,128)}) %reduce-scatter.2.cloned.1.call-update) | async-done | bytes 32784 | tf_op jit(solution)/shard_map/reduce_scatter | solution.py:75
  (18 shorter events, 0.1 us)
Async XLA Ops:
  7.2 2.9 %copy-start.3 = (f32[1,4,64,128]{3,2,1,0:T(8,128)S(1)}, f32[1,4,64,128]{3,2,1,0:T(8,128)}, u32[]{:S(2)}) copy-start(f32[1,4,64,128]{3,2,1,0:T(8,128)} %param.11) | copy-start | bytes 393220
  7.2 162.4 %reduce-scatter.2.cloned.1.call-start = ((), (), s32[]{:S(2)}) async-start(), calls=%async_computation.1 | async-start | bytes 163840 | tf_op jit(solution)/shard_map/reduce_scatter | solution.py:75
  10.1 12.7 %copy-start = (f32[1,16,4,64,128]{4,1,3,2,0:T(8,128)}, f32[1,16,4,64,128]{4,1,3,2,0:T(8,128)S(1)}, u32[]{:S(2)}) copy-start(f32[1,16,4,64,128]{4,1,3,2,0:T(8,128)S(1)} %copy.47) | copy-start | bytes 6291460
  10.3 27.7 %collective-permute-start = (f32[17,1,64,128]{3,2,1,0:T(8,128)S(1)}, f32[17,1,64,128]{3,2,1,0:T(8,128)}, u32[]{:S(2)}, u32[]{:S(2)}) collective-permute-start(f32[17,1,64,128]{3,2,1,0:T(8,128)S(1)} %copy.26), channel_id=1, source_target_pairs={{1,0},{2,1},{3,2},{4,3},{5,4},{6,5},{7,6},{0,7},{9,8},{10,9},{11,1... | collective-permute-start | bytes 1671176 | tf_op jit(solution)/shard_map/ppermute | solution.py:16
  17.3 3.0 %copy-start.12 = (f32[1,3,4,64,128]{4,3,2,1,0:T(8,128)S(1)}, f32[1,3,4,64,128]{4,3,2,1,0:T(8,128)}, u32[]{:S(2)}) copy-start(f32[1,3,4,64,128]{4,3,2,1,0:T(8,128)} %param.12) | copy-start | bytes 1179652
  17.3 22.1 %collective-permute-start.1 = (f32[17,1,64,128]{3,2,1,0:T(8,128)}, f32[17,1,64,128]{3,2,1,0:T(8,128)}, u32[]{:S(2)}, u32[]{:S(2)}) collective-permute-start(f32[17,1,64,128]{3,2,1,0:T(8,128)} %copy.28), channel_id=1, source_target_pairs={{0,1},{1,2},{2,3},{3,4},{4,5},{5,6},{6,7},{7,0},{8,9},{9,10},{10,1... | collective-permute-start | bytes 1671176 | tf_op jit(solution)/shard_map/ppermute | solution.py:15
  22.8 18.0 %copy-start.2 = (f32[17,4,63,128]{3,0,2,1:T(8,128)S(1)}, f32[17,4,63,128]{3,0,2,1:T(8,128)}, u32[]{:S(2)}) copy-start(f32[17,4,63,128]{3,0,2,1:T(8,128)} %get-tuple-element.54) | copy-start | bytes 6580228
  22.8 18.0 %copy-start.4 = (f32[4,64,128]{2,1,0:T(8,128)S(1)}, f32[4,64,128]{2,1,0:T(8,128)}, u32[]{:S(2)}) copy-start(f32[4,64,128]{2,1,0:T(8,128)} %get-tuple-element.62) | copy-start | bytes 393220
  22.8 18.0 %copy-start.8 = (f32[1,4,64,128]{3,2,1,0:T(8,128)S(1)}, f32[1,4,64,128]{3,2,1,0:T(8,128)}, u32[]{:S(2)}) copy-start(f32[1,4,64,128]{3,2,1,0:T(8,128)} %param.13) | copy-start | bytes 393220
  23.9 17.0 %copy-start.1 = (f32[1,16,4,64,128]{4,1,3,2,0:T(8,128)S(1)}, f32[1,16,4,64,128]{4,1,3,2,0:T(8,128)}, u32[]{:S(2)}) copy-start(f32[1,16,4,64,128]{4,1,3,2,0:T(8,128)} %copy-done) | copy-start | bytes 6291460
  40.9 5.6 %copy-start.10 = (f32[1,4,64,128]{3,2,1,0:T(8,128)S(1)}, f32[1,4,64,128]{3,2,1,0:T(8,128)}, u32[]{:S(2)}) copy-start(f32[1,4,64,128]{3,2,1,0:T(8,128)} %param.14) | copy-start | bytes 393220
  46.6 3.7 %copy-start.6 = (f32[1,4,64,128]{3,0,2,1:T(1,128)}, f32[1,4,64,128]{3,0,2,1:T(1,128)S(1)}, u32[]{:S(2)}) copy-start(f32[1,4,64,128]{3,0,2,1:T(1,128)S(1)} %slice_add_fusion.1) | copy-start | bytes 393220
  50.5 26.0 %collective-permute-start.2 = (f32[17,1,64,128]{3,2,1,0:T(8,128)S(1)}, f32[17,1,64,128]{3,2,1,0:T(8,128)S(1)}, u32[]{:S(2)}, u32[]{:S(2)}) collective-permute-start(f32[17,1,64,128]{3,2,1,0:T(8,128)S(1)} %copy.31), channel_id=1, source_target_pairs={{1,0},{2,1},{3,2},{4,3},{5,4},{6,5},{7,6},{0,7},{9,8},{10,9},{11,1... | collective-permute-start | bytes 1671176 | tf_op jit(solution)/shard_map/ppermute | solution.py:16
  55.4 22.4 %collective-permute-start.3 = (f32[17,1,64,128]{3,2,1,0:T(8,128)S(1)}, f32[17,1,64,128]{3,2,1,0:T(8,128)S(1)}, u32[]{:S(2)}, u32[]{:S(2)}) collective-permute-start(f32[17,1,64,128]{3,2,1,0:T(8,128)S(1)} %copy.33), channel_id=1, source_target_pairs={{0,1},{1,2},{2,3},{3,4},{4,5},{5,6},{6,7},{7,0},{8,9},{9,10},{10,1... | collective-permute-start | bytes 1671176 | tf_op jit(solution)/shard_map/ppermute | solution.py:15
  57.4 21.7 %copy-start.5 = (f32[4,64,128]{2,1,0:T(8,128)S(1)}, f32[4,64,128]{2,1,0:T(8,128)}, u32[]{:S(2)}) copy-start(f32[4,64,128]{2,1,0:T(8,128)} %get-tuple-element.62) | copy-start | bytes 393220
  57.4 21.7 %copy-start.9 = (f32[1,4,64,128]{3,2,1,0:T(8,128)S(1)}, f32[1,4,64,128]{3,2,1,0:T(8,128)}, u32[]{:S(2)}) copy-start(f32[1,4,64,128]{3,2,1,0:T(8,128)} %param.13) | copy-start | bytes 393220
  127.5 24.3 %copy-start.7 = (f32[1,4,64,128]{3,0,2,1:T(1,128)S(1)}, f32[1,4,64,128]{3,0,2,1:T(1,128)}, u32[]{:S(2)}) copy-start(f32[1,4,64,128]{3,0,2,1:T(1,128)} %copy-done.6) | copy-start | bytes 393220
  151.8 17.8 %copy-start.11 = (f32[32768]{0:T(1024)}, f32[32768]{0:T(1024)S(1)}, u32[]{:S(2)}) copy-start(f32[32768]{0:T(1024)S(1)} %sub.40) | copy-start | bytes 393220
Sparse Core Ops, SparseCore 0:
  152.6 16.8 reduce-scatter.1
